TPU v7x, 32 devices: a whole 2x2x4 slice. The times are simulated.
32 devices in a mesh: vol: 1, slab: 8 (over z, x), filt: 4 (over y, core).
Axes of the slice: x: 2, y: 2, z: 4, core: 2. Of those that a mesh axis runs over, the one named last changes fastest.
Arguments:
- volume: bfloat16 [32, 64, 64, 256], P(('vol', 'slab', 'filt')), may hold values from -6 to 6
- weights: bfloat16 [256, 27, 256], P('filt'), may hold values from -0.078125 to 0.078125
- bias: bfloat16 [256], P('filt'), may hold values from -3 to 3
Outputs:
- activated: bfloat16 [32, 64, 64, 256], P(('vol', 'slab'), None, None, 'filt')
All inputs are finite; a program needn't handle non-finite values.
Results may differ from a plain program's by a relative error of at most 0.001.
Values may be sent and summed in bfloat16 or wider, within the bound.
A program may use at most 448 MiB of HBM per device.

v0:
```python
import jax
import jax.numpy as jnp
from jax import lax
from jax.sharding import PartitionSpec as P


def extended(cells, sides, width):
    for axis, dim in sides:
        count = lax.axis_size(axis)
        ends = count - 1
        head = lax.slice_in_dim(cells, 0, width, axis=dim)
        tail = lax.slice_in_dim(cells, cells.shape[dim] - width, cells.shape[dim], axis=dim)
        cells = jnp.concatenate(
            [
                lax.ppermute(tail, axis, [(i, (i + 1) % count) for i in range(ends)]),
                cells,
                lax.ppermute(head, axis, [((i + 1) % count, i) for i in range(ends)]),
            ],
            axis=dim,
        )
    return cells


def convolve(padded, weights, bias):
    planes = padded.shape[0] - 2
    rows = padded.shape[1]
    cols = padded.shape[2]
    chans = padded.shape[3]
    outs = weights.shape[0]
    framed = jnp.pad(padded, ((0, 0), (1, 1), (1, 1), (0, 0)))
    total = jnp.zeros((planes, rows * cols, outs), jnp.float32)
    for tap_z in range(3):
        for tap_y in range(3):
            for tap_x in range(3):
                window = framed[
                    tap_z : tap_z + planes, tap_y : tap_y + rows, tap_x : tap_x + cols
                ].reshape(planes, rows * cols, chans)
                tap_weight = weights[:, 9 * tap_z + 3 * tap_y + tap_x, :]
                total = total + jnp.einsum(
                    "zpi,oi->zpo", window, tap_weight, preferred_element_type=jnp.float32
                )
    shifted = total + bias.astype(jnp.float32)[None, None, :]
    result = jnp.where(shifted > 0, shifted, 0.3 * shifted)
    return result.astype(jnp.bfloat16).reshape(planes, rows, cols, outs)


def body(volume, weights, bias):
    slab_planes = lax.all_gather(volume, "filt", axis=0, tiled=True)
    padded = extended(slab_planes, (("slab", 0),), 1)
    return convolve(padded, weights, bias)


def solution(mesh):
    return jax.shard_map(
        body,
        mesh=mesh,
        in_specs=(P(("vol", "slab", "filt"), None, None, None), P("filt", None, None), P("filt")),
        out_specs=P(("vol", "slab"), None, None, "filt"),
        check_vma=False,
    )
```

profile of v0, /device:TPU:0, one launch (start us, length us, event | category | flops | bytes accessed | tf_op | source)
XLA Modules:
  0.0 524.3 jit_solution(2084521685995472989)
XLA Ops:
  7.3 62.7 %all-gather.2.cloned.1.call-done = bf16[4,64,64,256]{3,2,1,0:T(8,128)(2,1)} async-done(((bf16[1,64,64,256]{3,2,1,0:T(8,128)(2,1)}), bf16[4,64,64,256]{3,2,1,0:T(8,128)(2,1)}) %all-gather.2.cloned.1.call-update) | async-done | bytes 8388624 | tf_op jit(solution)/shard_map/all_gather | solution.py:48
  78.4 4.6 fusion.57
  82.9 83.6 %collective-permute-done = bf16[1,64,64,256]{3,2,1,0:T(8,128)(2,1)S(1)} collective-permute-done((bf16[1,64,64,256]{3,2,1,0:T(8,128)(2,1)S(1)}, bf16[1,64,64,256]{3,2,1,0:T(8,128)(2,1)S(1)}, u32[]{:S(2)}, u32[]{:S(2)}) %collective-permute-start) | collective-permute-done | bytes 2097184 | tf_op jit(solution)/shard_map/ppermute | solution.py:15
  169.3 21.5 %select_maximum_fusion = bf16[6,66,66,256]{3,2,1,0:T(8,128)(2,1)} fusion(bf16[1,64,64,256]{3,2,1,0:T(8,128)(2,1)S(1)} %collective-permute-done.1, bf16[4,64,64,256]{3,2,1,0:T(8,128)(2,1)S(1)} %copy-done, bf16[1,64,64,256]{3,2,1,0:T(8,128)(2,1)S(1)} %collective-permute-done), kind=kLoop, calls=%fused_computation.7 | loop fusion | flops 127125504 | bytes 25964544 | tf_op jit(solution)/shard_map/concatenate | solution.py:13
  190.8 126.1 %fusion.111 = (bf16[4,64,64,256]{3,2,1,0:T(8,128)(2,1)}, bf16[4,64,64,256]{3,2,1,0:T(8,128)(2,1)}, bf16[4,64,64,256]{3,2,1,0:T(8,128)(2,1)}, bf16[4,64,64,256]{3...) fusion(bf16[6,66,66,256]{3,2,1,0:T(8,128)(2,1)} %select_maximum, ...), kind=kLoop, calls=%fused_computation.122 | loop fusion | bytes 318767104 | tf_op jit(solution)/shard_map/slice | solution.py:35
  316.9 32.3 %fusion.112 = (bf16[4,64,64,256]{3,2,1,0:T(8,128)(2,1)}, bf16[4,64,64,256]{3,2,1,0:T(8,128)(2,1)}, bf16[4,64,64,256]{3,2,1,0:T(8,128)(2,1)}, bf16[4,64,64,256]{3,2,1,0:T(8,128)(2,1)}, bf16[4,64,64,256]{3,2,1,0:T(8,128)(2,1)}) fusion(bf16[6,66,66,256]{3,2,1,0:T(8,128)(2,1)} %select_maximum_fusion), kind=kLoop, calls=%fused_computation.123 | loop fusion | bytes 83886080 | tf_op jit(solution)/shard_map/slice | solution.py:35
  349.2 8.2 %fusion.59 = f32[4,4096,64]{1,2,0:T(8,128)} fusion(bf16[4,4096,256]{2,1,0:T(8,128)(2,1)} %bitcast.221, bf16[64,27,256]{2,0,1:T(8,128)(2,1)S(1)} %copy-done.6), kind=kOutput, calls=%fused_computation.70 | convolution fusion | flops 536870912 | bytes 12615680 | tf_op jit(solution)/shard_map/zpi,oi->zpo/dot_general | solution.py:39
  357.4 4.6 fusion.61
  362.1 4.7 fusion.63
  366.8 4.6 fusion.65
  371.5 4.7 fusion.67
  376.1 4.6 fusion.69
  380.7 4.7 fusion.71
  385.4 4.6 fusion.73
  390.0 4.7 fusion.77
  394.8 4.6 fusion.79
  399.4 4.8 fusion.81
  408.6 4.6 fusion.75
  413.2 4.6 fusion.34
  417.8 4.6 fusion.36
  422.4 4.6 fusion.38
  431.6 4.6 fusion.44
  436.2 4.6 fusion.46
  440.8 4.6 fusion.48
  445.4 4.7 fusion.50
  450.2 4.6 fusion.52
  454.8 4.6 fusion.54
  459.3 4.7 fusion.32
  464.0 4.6 fusion.40
  468.6 24.2 %fusion.29 = f32[4,4096,64]{1,2,0:T(8,128)} fusion(f32[4,4096,64]{1,2,0:T(8,128)} %fusion.57, f32[4,4096,64]{1,2,0:T(8,128)} %fusion.59, f32[4,4096,64]{1,2,0:T(8,128)} %fusion.61, f32[4,4096,64]{1,2,0:T(8,128)} %fusion.63, f32[4,4096,64]{1,2,0:T(8,128)} %fusion.65, f32[4,4096,64]{1,2,0:T(8,128)} %fusion.67, f32[4,4096,64]{1,2,0:T(8,128)} %fusion.69, ...), kind=kOutput, calls=%fused_computation.40 | convolution fusion | flops 550502400 | bytes 67141632 | tf_op jit(solution)/shard_map/zpi,oi->zpo/dot_general | solution.py:39
  492.8 19.7 %fusion.31 = bf16[4,4096,64]{1,2,0:T(8,128)(2,1)} fusion(f32[4,4096,64]{1,2,0:T(8,128)} %fusion.32, f32[4,4096,64]{1,2,0:T(8,128)} %fusion.34, f32[4,4096,64]{1,2,0:T(8,128)} %fusion.36, f32[4,4096,64]{1,2,0:T(8,128)} %fusion.38, f32[4,4096,64]{1,2,0:T(8,128)} %fusion.40, f32[4,4096,64]{1,2,0:T(8,128)} %fusion.42, f32[4,4096,64]{1,2,0:T(8,128)} %fusion.44, ...), kind=kOutput, calls=%fused_computation.42 | convolution fusion | flops 555745280 | bytes 65044992 | tf_op jit(solution)/shard_map/zpi,oi->zpo/dot_general | solution.py:39
  512.5 4.8 copy.6
  (142 shorter events, 21.0 us)
Async XLA Ops:
  6.5 71.2 %copy-start.8 = (bf16[64]{0:T(256)(128)(2,1)S(1)}, bf16[64]{0:T(256)(128)(2,1)}, u32[]{:S(2)}) copy-start(bf16[64]{0:T(256)(128)(2,1)} %param.5) | copy-start | bytes 388
  6.5 71.8 %copy-start.6 = (bf16[64,27,256]{2,0,1:T(8,128)(2,1)S(1)}, bf16[64,27,256]{2,0,1:T(8,128)(2,1)}, u32[]{:S(2)}) copy-start(bf16[64,27,256]{2,0,1:T(8,128)(2,1)} %param.4) | copy-start | bytes 2654212
  6.5 63.4 %all-gather.2.cloned.1.call-start = ((), (), s32[]{:S(2)}) async-start(), calls=%async_computation | async-start | bytes 10485760 | tf_op jit(solution)/shard_map/all_gather | solution.py:48
  69.9 8.4 %copy-start = (bf16[4,64,64,256]{3,2,1,0:T(8,128)(2,1)S(1)}, bf16[4,64,64,256]{3,2,1,0:T(8,128)(2,1)}, u32[]{:S(2)}) copy-start(bf16[4,64,64,256]{3,2,1,0:T(8,128)(2,1)} %all-gather.2.cloned.1.call-done) | copy-start | bytes 25165828
  72.8 93.7 %collective-permute-start = (bf16[1,64,64,256]{3,2,1,0:T(8,128)(2,1)S(1)}, bf16[1,64,64,256]{3,2,1,0:T(8,128)(2,1)S(1)}, u32[]{:S(2)}, u32[]{:S(2)}) collective-permute-start(bf16[1,64,64,256]{3,2,1,0:T(8,128)(2,1)S(1)} %get-tuple-element.31), channel_id=1, source_target_pairs={{0,4},{4,8},{8,12},{12,16},{16,20},{20,24},{24,28},{1,5},{5,9},{9,... | collective-permute-start | bytes 6291464 | tf_op jit(solution)/shard_map/ppermute | solution.py:15
  76.5 90.1 %collective-permute-start.1 = (bf16[1,64,64,256]{3,2,1,0:T(8,128)(2,1)S(1)}, bf16[1,64,64,256]{3,2,1,0:T(8,128)(2,1)S(1)}, u32[]{:S(2)}, u32[]{:S(2)}) collective-permute-start(bf16[1,64,64,256]{3,2,1,0:T(8,128)(2,1)S(1)} %get-tuple-element.32), channel_id=1, source_target_pairs={{4,0},{8,4},{12,8},{16,12},{20,16},{24,20},{28,24},{5,1},{9,5},{13... | collective-permute-start | bytes 6291464 | tf_op jit(solution)/shard_map/ppermute | solution.py:17
  349.2 12.8 %slice-start.34 = ((s8[8388608]{0:T(1024)(128)(4,1)}), s8[4194304]{0:T(1024)(128)(4,1)S(1)}, s32[]{:S(2)}) async-start(s8[8388608]{0:T(1024)(128)(4,1)} %bitcast.214), calls=%async_computation.35 | async-start | bytes 8388608
  357.4 9.4 %slice-start.32 = ((s8[8388608]{0:T(1024)(128)(4,1)}), s8[4194304]{0:T(1024)(128)(4,1)S(1)}, s32[]{:S(2)}) async-start(s8[8388608]{0:T(1024)(128)(4,1)} %bitcast.211), calls=%async_computation.33 | async-start | bytes 8388608
  362.1 9.4 %slice-start.30 = ((s8[8388608]{0:T(1024)(128)(4,1)}), s8[4194304]{0:T(1024)(128)(4,1)S(1)}, s32[]{:S(2)}) async-start(s8[8388608]{0:T(1024)(128)(4,1)} %bitcast.208), calls=%async_computation.31 | async-start | bytes 8388608
  366.8 9.3 %slice-start.28 = ((s8[8388608]{0:T(1024)(128)(4,1)}), s8[4194304]{0:T(1024)(128)(4,1)S(1)}, s32[]{:S(2)}) async-start(s8[8388608]{0:T(1024)(128)(4,1)} %bitcast.205), calls=%async_computation.29 | async-start | bytes 8388608
  371.5 9.3 %slice-start.26 = ((s8[8388608]{0:T(1024)(128)(4,1)}), s8[4194304]{0:T(1024)(128)(4,1)S(1)}, s32[]{:S(2)}) async-start(s8[8388608]{0:T(1024)(128)(4,1)} %bitcast.202), calls=%async_computation.27 | async-start | bytes 8388608
  376.1 9.3 %slice-start.24 = ((s8[8388608]{0:T(1024)(128)(4,1)}), s8[4194304]{0:T(1024)(128)(4,1)S(1)}, s32[]{:S(2)}) async-start(s8[8388608]{0:T(1024)(128)(4,1)} %bitcast.199), calls=%async_computation.25 | async-start | bytes 8388608
  380.7 9.3 %slice-start.42 = ((s8[8388608]{0:T(1024)(128)(4,1)}), s8[4194304]{0:T(1024)(128)(4,1)S(1)}, s32[]{:S(2)}) async-start(s8[8388608]{0:T(1024)(128)(4,1)} %bitcast.228), calls=%async_computation.43 | async-start | bytes 8388608
  385.4 9.4 %slice-start.40 = ((s8[8388608]{0:T(1024)(128)(4,1)}), s8[4194304]{0:T(1024)(128)(4,1)S(1)}, s32[]{:S(2)}) async-start(s8[8388608]{0:T(1024)(128)(4,1)} %bitcast.225), calls=%async_computation.41 | async-start | bytes 8388608
  390.0 9.4 %slice-start.38 = ((s8[8388608]{0:T(1024)(128)(4,1)}), s8[4194304]{0:T(1024)(128)(4,1)S(1)}, s32[]{:S(2)}) async-start(s8[8388608]{0:T(1024)(128)(4,1)} %bitcast.222), calls=%async_computation.39 | async-start | bytes 8388608
  394.8 9.4 %slice-start = ((s8[8388608]{0:T(1024)(128)(4,1)}), s8[4194304]{0:T(1024)(128)(4,1)S(1)}, s32[]{:S(2)}) async-start(s8[8388608]{0:T(1024)(128)(4,1)} %bitcast.164), calls=%async_computation.1 | async-start | bytes 8388608
  399.4 13.8 %slice-start.22 = ((s8[8388608]{0:T(1024)(128)(4,1)}), s8[4194304]{0:T(1024)(128)(4,1)S(1)}, s32[]{:S(2)}) async-start(s8[8388608]{0:T(1024)(128)(4,1)} %bitcast.196), calls=%async_computation.23 | async-start | bytes 8388608
  404.2 9.0 %slice-start.23 = ((s8[8388608]{0:T(1024)(128)(4,1)}), s8[4194304]{0:T(1024)(128)(4,1)S(1)}, s32[]{:S(2)}) async-start(s8[8388608]{0:T(1024)(128)(4,1)} %bitcast.196), calls=%async_computation.24 | async-start | bytes 8388608
  408.6 9.2 %slice-start.20 = ((s8[8388608]{0:T(1024)(128)(4,1)}), s8[4194304]{0:T(1024)(128)(4,1)S(1)}, s32[]{:S(2)}) async-start(s8[8388608]{0:T(1024)(128)(4,1)} %bitcast.193), calls=%async_computation.21 | async-start | bytes 8388608
  413.2 9.2 %slice-start.18 = ((s8[8388608]{0:T(1024)(128)(4,1)}), s8[4194304]{0:T(1024)(128)(4,1)S(1)}, s32[]{:S(2)}) async-start(s8[8388608]{0:T(1024)(128)(4,1)} %bitcast.190), calls=%async_computation.19 | async-start | bytes 8388608
  417.8 9.2 %slice-start.16 = ((s8[8388608]{0:T(1024)(128)(4,1)}), s8[4194304]{0:T(1024)(128)(4,1)S(1)}, s32[]{:S(2)}) async-start(s8[8388608]{0:T(1024)(128)(4,1)} %bitcast.187), calls=%async_computation.17 | async-start | bytes 8388608
  422.4 9.2 %slice-start.14 = ((s8[8388608]{0:T(1024)(128)(4,1)}), s8[4194304]{0:T(1024)(128)(4,1)S(1)}, s32[]{:S(2)}) async-start(s8[8388608]{0:T(1024)(128)(4,1)} %bitcast.184), calls=%async_computation.15 | async-start | bytes 8388608
  427.0 9.2 %slice-start.10 = ((s8[8388608]{0:T(1024)(128)(4,1)}), s8[4194304]{0:T(1024)(128)(4,1)S(1)}, s32[]{:S(2)}) async-start(s8[8388608]{0:T(1024)(128)(4,1)} %bitcast.178), calls=%async_computation.11 | async-start | bytes 8388608
  431.6 9.2 %slice-start.8 = ((s8[8388608]{0:T(1024)(128)(4,1)}), s8[4194304]{0:T(1024)(128)(4,1)S(1)}, s32[]{:S(2)}) async-start(s8[8388608]{0:T(1024)(128)(4,1)} %bitcast.175), calls=%async_computation.9 | async-start | bytes 8388608
  436.2 9.2 %slice-start.6 = ((s8[8388608]{0:T(1024)(128)(4,1)}), s8[4194304]{0:T(1024)(128)(4,1)S(1)}, s32[]{:S(2)}) async-start(s8[8388608]{0:T(1024)(128)(4,1)} %bitcast.172), calls=%async_computation.7 | async-start | bytes 8388608
  440.8 9.3 %slice-start.4 = ((s8[8388608]{0:T(1024)(128)(4,1)}), s8[4194304]{0:T(1024)(128)(4,1)S(1)}, s32[]{:S(2)}) async-start(s8[8388608]{0:T(1024)(128)(4,1)} %bitcast.169), calls=%async_computation.5 | async-start | bytes 8388608
  445.4 9.4 %slice-start.2 = ((s8[8388608]{0:T(1024)(128)(4,1)}), s8[4194304]{0:T(1024)(128)(4,1)S(1)}, s32[]{:S(2)}) async-start(s8[8388608]{0:T(1024)(128)(4,1)} %bitcast.166), calls=%async_computation.3 | async-start | bytes 8388608
  450.2 9.2 %slice-start.12 = ((s8[8388608]{0:T(1024)(128)(4,1)}), s8[4194304]{0:T(1024)(128)(4,1)S(1)}, s32[]{:S(2)}) async-start(s8[8388608]{0:T(1024)(128)(4,1)} %bitcast.181), calls=%async_computation.13 | async-start | bytes 8388608
  454.8 9.2 %slice-start.36 = ((s8[8388608]{0:T(1024)(128)(4,1)}), s8[4194304]{0:T(1024)(128)(4,1)S(1)}, s32[]{:S(2)}) async-start(s8[8388608]{0:T(1024)(128)(4,1)} %bitcast.217), calls=%async_computation.37 | async-start | bytes 8388608
  464.0 28.8 %slice-start.44 = ((s8[8388608]{0:T(1024)(128)(4,1)}), s8[4194304]{0:T(1024)(128)(4,1)S(1)}, s32[]{:S(2)}) async-start(s8[8388608]{0:T(1024)(128)(4,1)} %bitcast.232), calls=%async_computation.45 | async-start | bytes 8388608
  468.6 24.2 %slice-start.45 = ((s8[8388608]{0:T(1024)(128)(4,1)}), s8[4194304]{0:T(1024)(128)(4,1)S(1)}, s32[]{:S(2)}) async-start(s8[8388608]{0:T(1024)(128)(4,1)} %bitcast.232), calls=%async_computation.46 | async-start | bytes 8388608
  468.6 24.2 %copy-start.7 = (f32[64]{0:T(128)S(1)}, f32[64]{0:T(128)}, u32[]{:S(2)}) copy-start(f32[64]{0:T(128)} %convert_element_type.8) | copy-start | bytes 772
  (26 other events, 118.1 us)
Sparse Core Ops, SparseCore 0:
  8.9 60.9 all-gather.1
where the time goes:
time: 527 us; the launch traced here: 524 us
  local copies, waits for them, and re-layouts  169 us (32%)
  matrix products  163 us (31%)
  waiting for transfers between devices  147 us (28%)
  other arithmetic  26.5 us (5%)
  between operations  14 us (3%)
    dot_general x27, matrix products, convolve(): jnp.einsum('zpi,oi->zpo', window, tap_weight, preferred_element_type=jnp....  163 us
    slice x2, local copies, waits for them, and re-layouts, convolve(): framed[tap_z:tap_z + planes, tap_y:tap_y + rows, tap_x:tap_x + cols]  158 us
    ppermute x1, waiting for transfers between devices, extended(): lax.ppermute(tail, axis, [(i, (i + 1) % count) for i in range(ends)])  83.6 us
    all_gather x1, waiting for transfers between devices, body(): slab_planes = lax.all_gather(volume, 'filt', axis=0, tiled=True)  62.7 us
    concatenate x2, other arithmetic, extended(): jnp.concatenate([lax.ppermute(tail, axis, [(i, (i + 1) % count) for i in...  25.9 us
  transfers between devices with their start and end apart: 3, of which 2 were waited for; matrix products, arithmetic and copies ran while one was open for 1% of the time, Pallas kernels for 0%

commit v1 on v0

--- a/solution.py
+++ b/solution.py
@@ -45,7 +45,15 @@
 
 
 def body(volume, weights, bias):
-    slab_planes = lax.all_gather(volume, "filt", axis=0, tiled=True)
+    ways, here, step = (lax.axis_size("filt"), lax.axis_index("filt"), volume.shape[0])
+    line, have = (volume, 1)
+    while have < ways:
+        line = jnp.concatenate(
+            [line, lax.ppermute(line, "filt", [(d, (d - have) % ways) for d in range(ways)])],
+            axis=0,
+        )
+        have = 2 * have
+    slab_planes = jnp.roll(line, here * step, axis=0)
     padded = extended(slab_planes, (("slab", 0),), 1)
     return convolve(padded, weights, bias)
 

time: 527 us -> 585 us (1.11)
  waiting for transfers between devices: 147 us -> 186 us
  local copies, waits for them, and re-layouts: 169 us -> 191 us
  between operations: 14 us -> 0.63 us
    ppermute x0 -> x2, waiting for transfers between devices: none -> 115 us  [body(): lax.ppermute(line, 'filt', [(d, (d - have) % ways) for d in range(ways)])]
    all_gather x1 -> x0, waiting for transfers between devices: 62.7 us -> none  [body(): slab_planes = lax.all_gather(volume, 'filt', axis=0, tiled=True)]
    ppermute x1, waiting for transfers between devices: 83.6 us -> 71.6 us  [extended(): lax.ppermute(tail, axis, [(i, (i + 1) % count) for i in range(ends)])]
    unnamed x110 -> x113, local copies, waits for them, and re-layouts: 2.95 us -> 13.5 us
    dynamic_slice x0 -> x1, local copies, waits for them, and re-layouts: none -> 8.36 us  [body(): slab_planes = jnp.roll(line, here * step, axis=0)]
  transfers between devices with their start and end apart: 3 -> 4, of which waited for: 2 -> 3; matrix products, arithmetic and copies ran while one was open for 1% -> 3% of each run, Pallas kernels for 0% -> 0%
where the time goes in v1:
time: 585 us; the launch traced here: 582 us
  local copies, waits for them, and re-layouts  191 us (33%)
  waiting for transfers between devices  186 us (32%)
  matrix products  164 us (28%)
  other arithmetic  31.7 us (5%)
  starting transfers between devices  8.03 us (1%)
    dot_general x27, matrix products, convolve(): jnp.einsum('zpi,oi->zpo', window, tap_weight, preferred_element_type=jnp....  164 us
    slice x2, local copies, waits for them, and re-layouts, convolve(): framed[tap_z:tap_z + planes, tap_y:tap_y + rows, tap_x:tap_x + cols]  161 us
    ppermute x2, waiting for transfers between devices, body(): lax.ppermute(line, 'filt', [(d, (d - have) % ways) for d in range(ways)])  115 us
    ppermute x1, waiting for transfers between devices, extended(): lax.ppermute(tail, axis, [(i, (i + 1) % count) for i in range(ends)])  71.6 us
    concatenate x2, other arithmetic, extended(): jnp.concatenate([lax.ppermute(tail, axis, [(i, (i + 1) % count) for i in...  27.2 us
    unnamed x113, local copies, waits for them, and re-layouts  13.5 us
  transfers between devices with their start and end apart: 4, of which 3 were waited for; matrix products, arithmetic and copies ran while one was open for 3% of the time, Pallas kernels for 0%

profile of v1, /device:TPU:0, one launch (start us, length us, event | category | flops | bytes accessed | tf_op | source)
XLA Modules:
  0.0 582.0 jit_solution(15041806501074869368)
XLA Ops:
  2.4 23.9 %collective-permute-done = bf16[1,64,64,256]{3,2,1,0:T(8,128)(2,1)S(1)} collective-permute-done((bf16[1,64,64,256]{3,2,1,0:T(8,128)(2,1)}, bf16[1,64,64,256]{3,2,1,0:T(8,128)(2,1)S(1)}, u32[]{:S(2)}, u32[]{:S(2)}) %collective-permute-start) | collective-permute-done | bytes 2097184 | tf_op jit(solution)/shard_map/ppermute | solution.py:52
  34.3 90.9 %collective-permute-done.1 = bf16[2,64,64,256]{3,2,1,0:T(8,128)(2,1)} collective-permute-done((bf16[2,64,64,256]{3,2,1,0:T(8,128)(2,1)}, bf16[2,64,64,256]{3,2,1,0:T(8,128)(2,1)}, u32[]{:S(2)}, u32[]{:S(2)}) %collective-permute-start.1) | collective-permute-done | bytes 4194336 | tf_op jit(solution)/shard_map/ppermute | solution.py:52
  130.6 5.8 copy-done.4
  144.3 8.4 %constant_dynamic-slice_fusion.2 = bf16[4,64,64,256]{3,2,1,0:T(8,128)(2,1)} fusion(bf16[8,64,64,256]{3,2,1,0:T(8,128)(2,1)} %copy-done.4, s32[]{:T(128)S(6)} %select_n.18), kind=kLoop, calls=%fused_computation.132 | loop fusion | bytes 16777220 | tf_op jit(solution)/shard_map/jit(_roll_dynamic)/dynamic_slice | solution.py:56
  152.7 8.1 %fusion.59 = f32[4,4096,64]{1,2,0:T(8,128)} fusion(bf16[4,4096,256]{2,1,0:T(8,128)(2,1)} %bitcast.163, bf16[64,27,256]{2,0,1:T(8,128)(2,1)S(1)} %copy-done.7), kind=kOutput, calls=%fused_computation.70 | convolution fusion | flops 536870912 | bytes 12615680 | tf_op jit(solution)/shard_map/zpi,oi->zpo/dot_general | solution.py:39
  160.8 71.6 %collective-permute-done.2 = bf16[1,64,64,256]{3,2,1,0:T(8,128)(2,1)S(1)} collective-permute-done((bf16[1,64,64,256]{3,2,1,0:T(8,128)(2,1)}, bf16[1,64,64,256]{3,2,1,0:T(8,128)(2,1)S(1)}, u32[]{:S(2)}, u32[]{:S(2)}) %collective-permute-start.2) | collective-permute-done | bytes 2097184 | tf_op jit(solution)/shard_map/ppermute | solution.py:15
  233.7 21.4 %select_maximum_fusion = bf16[6,66,66,256]{3,2,1,0:T(8,128)(2,1)} fusion(bf16[1,64,64,256]{3,2,1,0:T(8,128)(2,1)S(1)} %collective-permute-done.3, bf16[4,64,64,256]{3,2,1,0:T(8,128)(2,1)S(1)} %copy-done, bf16[1,64,64,256]{3,2,1,0:T(8,128)(2,1)S(1)} %collective-permute-done.2), kind=kLoop, calls=%fused_computation.7 | loop fusion | flops 127125504 | bytes 25964544 | tf_op jit(solution)/shard_map/concatenate | solution.py:13
  255.1 125.7 %fusion.113 = (bf16[4,64,64,256]{3,2,1,0:T(8,128)(2,1)}, bf16[4,64,64,256]{3,2,1,0:T(8,128)(2,1)}, bf16[4,64,64,256]{3,2,1,0:T(8,128)(2,1)}, bf16[4,64,64,256]{3...) fusion(bf16[6,66,66,256]{3,2,1,0:T(8,128)(2,1)} %select_maximum, ...), kind=kLoop, calls=%fused_computation.133 | loop fusion | bytes 318767104 | tf_op jit(solution)/shard_map/slice | solution.py:35
  380.8 35.6 %fusion.114 = (bf16[4,64,64,256]{3,2,1,0:T(8,128)(2,1)}, bf16[4,64,64,256]{3,2,1,0:T(8,128)(2,1)}, bf16[4,64,64,256]{3,2,1,0:T(8,128)(2,1)}, bf16[4,64,64,256]{3,2,1,0:T(8,128)(2,1)}, bf16[4,64,64,256]{3,2,1,0:T(8,128)(2,1)}) fusion(bf16[6,66,66,256]{3,2,1,0:T(8,128)(2,1)} %select_maximum_fusion), kind=kLoop, calls=%fused_computation.134 | loop fusion | bytes 83886080 | tf_op jit(solution)/shard_map/slice | solution.py:35
  416.4 5.8 pad_maximum_fusion.1
  426.8 4.6 fusion.77
  431.4 4.6 fusion.35
  436.0 4.6 fusion.37
  440.7 4.6 fusion.39
  445.3 4.6 fusion.43
  450.0 4.6 fusion.45
  454.6 4.6 fusion.47
  459.2 4.9 fusion.49
  464.1 4.6 fusion.51
  468.8 4.6 fusion.53
  478.0 4.7 fusion.57
  482.7 4.6 fusion.61
  487.3 4.6 fusion.63
  496.5 4.6 fusion.67
  501.1 4.8 fusion.69
  510.5 4.7 fusion.73
  515.2 8.2 %fusion.33 = f32[4,4096,64]{1,2,0:T(8,128)} fusion(bf16[4,4096,256]{2,1,0:T(8,128)(2,1)} %bitcast.182, bf16[64,27,256]{2,0,1:T(8,128)(2,1)S(1)} %copy-done.7), kind=kOutput, calls=%fused_computation.44 | convolution fusion | flops 536870912 | bytes 12615680 | tf_op jit(solution)/shard_map/zpi,oi->zpo/dot_general | solution.py:39
  523.4 4.6 fusion.75
  528.0 4.6 fusion.79
  532.6 4.6 fusion.81
  537.2 4.7 fusion.83
  541.9 36.7 %fusion.32 = bf16[4,4096,64]{1,2,0:T(8,128)(2,1)S(1)} fusion(f32[4,4096,64]{1,2,0:T(8,128)} %fusion.33, f32[4,4096,64]{1,2,0:T(8,128)} %fusion.35, f32[4,4096,64]{1,2,0:T(8,128)} %fusion.37, f32[4,4096,64]{1,2,0:T(8,128)} %fusion.39, f32[4,4096,64]{1,2,0:T(8,128)} %fusion.41, f32[4,4096,64]{1,2,0:T(8,128)} %fusion.43, f32[4,4096,64]{1,2,0:T(8,128)} %fusion.45, ...), kind=kOutput, calls=%fused_computation.42 | convolution fusion | flops 569376768 | bytes 119570944 | tf_op jit(solution)/shard_map/zpi,oi->zpo/dot_general | solution.py:39
  (148 shorter events, 46.6 us)
Async XLA Ops:
  0.0 32.2 %copy-start.1 = (bf16[1,64,64,256]{3,2,1,0:T(8,128)(2,1)S(1)}, bf16[1,64,64,256]{3,2,1,0:T(8,128)(2,1)}, u32[]{:S(2)}) copy-start(bf16[1,64,64,256]{3,2,1,0:T(8,128)(2,1)} %param.3) | copy-start | bytes 6291460
  0.0 26.3 %collective-permute-start = (bf16[1,64,64,256]{3,2,1,0:T(8,128)(2,1)}, bf16[1,64,64,256]{3,2,1,0:T(8,128)(2,1)S(1)}, u32[]{:S(2)}, u32[]{:S(2)}) collective-permute-start(bf16[1,64,64,256]{3,2,1,0:T(8,128)(2,1)} %param.3), channel_id=1, source_target_pairs={{0,3},{1,0},{2,1},{3,2},{4,7},{5,4},{6,5},{7,6},{8,11},{9,8},{10,9... | collective-permute-start | bytes 6291464 | tf_op jit(solution)/shard_map/ppermute | solution.py:52
  31.6 93.6 %collective-permute-start.1 = (bf16[2,64,64,256]{3,2,1,0:T(8,128)(2,1)}, bf16[2,64,64,256]{3,2,1,0:T(8,128)(2,1)}, u32[]{:S(2)}, u32[]{:S(2)}) collective-permute-start(bf16[2,64,64,256]{3,2,1,0:T(8,128)(2,1)} %pad_maximum_fusion.2), channel_id=1, source_target_pairs={{0,2},{1,3},{2,0},{3,1},{4,6},{5,7},{6,4},{7,5},{8,10},{9,11},{10,... | collective-permute-start | bytes 12582920 | tf_op jit(solution)/shard_map/ppermute | solution.py:52
  32.4 95.5 %copy-start.3 = (bf16[1,64,64,256]{3,2,1,0:T(8,128)(2,1)S(1)}, bf16[1,64,64,256]{3,2,1,0:T(8,128)(2,1)}, u32[]{:S(2)}) copy-start(bf16[1,64,64,256]{3,2,1,0:T(8,128)(2,1)} %copy-done.2) | copy-start | bytes 6291460
  128.1 15.7 %copy-start.9 = (bf16[64]{0:T(256)(128)(2,1)S(1)}, bf16[64]{0:T(256)(128)(2,1)}, u32[]{:S(2)}) copy-start(bf16[64]{0:T(256)(128)(2,1)} %param.5) | copy-start | bytes 388
  138.8 93.6 %collective-permute-start.2 = (bf16[1,64,64,256]{3,2,1,0:T(8,128)(2,1)}, bf16[1,64,64,256]{3,2,1,0:T(8,128)(2,1)S(1)}, u32[]{:S(2)}, u32[]{:S(2)}) collective-permute-start(bf16[1,64,64,256]{3,2,1,0:T(8,128)(2,1)} %get-tuple-element.5), channel_id=1, source_target_pairs={{0,4},{4,8},{8,12},{12,16},{16,20},{20,24},{24,28},{1,5},{5,9},{9,... | collective-permute-start | bytes 6291464 | tf_op jit(solution)/shard_map/ppermute | solution.py:15
  142.3 90.1 %collective-permute-start.3 = (bf16[1,64,64,256]{3,2,1,0:T(8,128)(2,1)}, bf16[1,64,64,256]{3,2,1,0:T(8,128)(2,1)S(1)}, u32[]{:S(2)}, u32[]{:S(2)}) collective-permute-start(bf16[1,64,64,256]{3,2,1,0:T(8,128)(2,1)} %get-tuple-element.6), channel_id=1, source_target_pairs={{4,0},{8,4},{12,8},{16,12},{20,16},{24,20},{28,24},{5,1},{9,5},{13... | collective-permute-start | bytes 6291464 | tf_op jit(solution)/shard_map/ppermute | solution.py:17
  144.3 8.4 %copy-start.7 = (bf16[64,27,256]{2,0,1:T(8,128)(2,1)S(1)}, bf16[64,27,256]{2,0,1:T(8,128)(2,1)}, u32[]{:S(2)}) copy-start(bf16[64,27,256]{2,0,1:T(8,128)(2,1)} %param.4) | copy-start | bytes 2654212
  152.7 81.0 %copy-start = (bf16[4,64,64,256]{3,2,1,0:T(8,128)(2,1)S(1)}, bf16[4,64,64,256]{3,2,1,0:T(8,128)(2,1)}, u32[]{:S(2)}) copy-start(bf16[4,64,64,256]{3,2,1,0:T(8,128)(2,1)} %constant_dynamic-slice_fusion.2) | copy-start | bytes 25165828
  380.8 35.6 %copy-start.6 = (bf16[1,64,64,256]{3,2,1,0:T(8,128)(2,1)S(1)}, bf16[1,64,64,256]{3,2,1,0:T(8,128)(2,1)}, u32[]{:S(2)}) copy-start(bf16[1,64,64,256]{3,2,1,0:T(8,128)(2,1)} %copy-done.5) | copy-start | bytes 6291460
  422.2 9.2 %slice-start.42 = ((s8[8388608]{0:T(1024)(128)(4,1)}), s8[4194304]{0:T(1024)(128)(4,1)S(1)}, s32[]{:S(2)}) async-start(s8[8388608]{0:T(1024)(128)(4,1)} %bitcast.228), calls=%async_computation.42 | async-start | bytes 8388608
  426.8 9.2 %slice-start.40 = ((s8[8388608]{0:T(1024)(128)(4,1)}), s8[4194304]{0:T(1024)(128)(4,1)S(1)}, s32[]{:S(2)}) async-start(s8[8388608]{0:T(1024)(128)(4,1)} %bitcast.225), calls=%async_computation.40 | async-start | bytes 8388608
  431.4 9.2 %slice-start.38 = ((s8[8388608]{0:T(1024)(128)(4,1)}), s8[4194304]{0:T(1024)(128)(4,1)S(1)}, s32[]{:S(2)}) async-start(s8[8388608]{0:T(1024)(128)(4,1)} %bitcast.222), calls=%async_computation.38 | async-start | bytes 8388608
  436.0 9.3 %slice-start.36 = ((s8[8388608]{0:T(1024)(128)(4,1)}), s8[4194304]{0:T(1024)(128)(4,1)S(1)}, s32[]{:S(2)}) async-start(s8[8388608]{0:T(1024)(128)(4,1)} %bitcast.219), calls=%async_computation.36 | async-start | bytes 8388608
  440.6 9.3 %slice-start.34 = ((s8[8388608]{0:T(1024)(128)(4,1)}), s8[4194304]{0:T(1024)(128)(4,1)S(1)}, s32[]{:S(2)}) async-start(s8[8388608]{0:T(1024)(128)(4,1)} %bitcast.216), calls=%async_computation.34 | async-start | bytes 8388608
  445.3 9.2 %slice-start.32 = ((s8[8388608]{0:T(1024)(128)(4,1)}), s8[4194304]{0:T(1024)(128)(4,1)S(1)}, s32[]{:S(2)}) async-start(s8[8388608]{0:T(1024)(128)(4,1)} %bitcast.213), calls=%async_computation.32 | async-start | bytes 8388608
  450.0 9.3 %slice-start.30 = ((s8[8388608]{0:T(1024)(128)(4,1)}), s8[4194304]{0:T(1024)(128)(4,1)S(1)}, s32[]{:S(2)}) async-start(s8[8388608]{0:T(1024)(128)(4,1)} %bitcast.210), calls=%async_computation.30 | async-start | bytes 8388608
  454.6 9.5 %slice-start.28 = ((s8[8388608]{0:T(1024)(128)(4,1)}), s8[4194304]{0:T(1024)(128)(4,1)S(1)}, s32[]{:S(2)}) async-start(s8[8388608]{0:T(1024)(128)(4,1)} %bitcast.207), calls=%async_computation.28 | async-start | bytes 8388608
  459.2 9.5 %slice-start.26 = ((s8[8388608]{0:T(1024)(128)(4,1)}), s8[4194304]{0:T(1024)(128)(4,1)S(1)}, s32[]{:S(2)}) async-start(s8[8388608]{0:T(1024)(128)(4,1)} %bitcast.204), calls=%async_computation.26 | async-start | bytes 8388608
  464.1 9.2 %slice-start.24 = ((s8[8388608]{0:T(1024)(128)(4,1)}), s8[4194304]{0:T(1024)(128)(4,1)S(1)}, s32[]{:S(2)}) async-start(s8[8388608]{0:T(1024)(128)(4,1)} %bitcast.201), calls=%async_computation.24 | async-start | bytes 8388608
  468.7 9.2 %slice-start.22 = ((s8[8388608]{0:T(1024)(128)(4,1)}), s8[4194304]{0:T(1024)(128)(4,1)S(1)}, s32[]{:S(2)}) async-start(s8[8388608]{0:T(1024)(128)(4,1)} %bitcast.198), calls=%async_computation.22 | async-start | bytes 8388608
  473.4 9.3 %slice-start.20 = ((s8[8388608]{0:T(1024)(128)(4,1)}), s8[4194304]{0:T(1024)(128)(4,1)S(1)}, s32[]{:S(2)}) async-start(s8[8388608]{0:T(1024)(128)(4,1)} %bitcast.195), calls=%async_computation.20 | async-start | bytes 8388608
  478.0 9.3 %slice-start.18 = ((s8[8388608]{0:T(1024)(128)(4,1)}), s8[4194304]{0:T(1024)(128)(4,1)S(1)}, s32[]{:S(2)}) async-start(s8[8388608]{0:T(1024)(128)(4,1)} %bitcast.192), calls=%async_computation.18 | async-start | bytes 8388608
  482.7 9.2 %slice-start.16 = ((s8[8388608]{0:T(1024)(128)(4,1)}), s8[4194304]{0:T(1024)(128)(4,1)S(1)}, s32[]{:S(2)}) async-start(s8[8388608]{0:T(1024)(128)(4,1)} %bitcast.189), calls=%async_computation.16 | async-start | bytes 8388608
  487.3 9.2 %slice-start.14 = ((s8[8388608]{0:T(1024)(128)(4,1)}), s8[4194304]{0:T(1024)(128)(4,1)S(1)}, s32[]{:S(2)}) async-start(s8[8388608]{0:T(1024)(128)(4,1)} %bitcast.186), calls=%async_computation.14 | async-start | bytes 8388608
  491.9 9.2 %slice-start.12 = ((s8[8388608]{0:T(1024)(128)(4,1)}), s8[4194304]{0:T(1024)(128)(4,1)S(1)}, s32[]{:S(2)}) async-start(s8[8388608]{0:T(1024)(128)(4,1)} %bitcast.183), calls=%async_computation.12 | async-start | bytes 8388608
  496.5 9.5 %slice-start.10 = ((s8[8388608]{0:T(1024)(128)(4,1)}), s8[4194304]{0:T(1024)(128)(4,1)S(1)}, s32[]{:S(2)}) async-start(s8[8388608]{0:T(1024)(128)(4,1)} %bitcast.179), calls=%async_computation.10 | async-start | bytes 8388608
  501.1 9.4 %slice-start.6 = ((s8[8388608]{0:T(1024)(128)(4,1)}), s8[4194304]{0:T(1024)(128)(4,1)S(1)}, s32[]{:S(2)}) async-start(s8[8388608]{0:T(1024)(128)(4,1)} %bitcast.173), calls=%async_computation.6 | async-start | bytes 8388608
  510.5 12.8 %slice-start.8 = ((s8[8388608]{0:T(1024)(128)(4,1)}), s8[4194304]{0:T(1024)(128)(4,1)S(1)}, s32[]{:S(2)}) async-start(s8[8388608]{0:T(1024)(128)(4,1)} %bitcast.176), calls=%async_computation.8 | async-start | bytes 8388608
  515.2 12.8 %slice-start.4 = ((s8[8388608]{0:T(1024)(128)(4,1)}), s8[4194304]{0:T(1024)(128)(4,1)S(1)}, s32[]{:S(2)}) async-start(s8[8388608]{0:T(1024)(128)(4,1)} %bitcast.170), calls=%async_computation.4 | async-start | bytes 8388608
  523.4 9.2 %slice-start.2 = ((s8[8388608]{0:T(1024)(128)(4,1)}), s8[4194304]{0:T(1024)(128)(4,1)S(1)}, s32[]{:S(2)}) async-start(s8[8388608]{0:T(1024)(128)(4,1)} %bitcast.167), calls=%async_computation.2 | async-start | bytes 8388608
  528.0 9.3 %slice-start = ((s8[8388608]{0:T(1024)(128)(4,1)}), s8[4194304]{0:T(1024)(128)(4,1)S(1)}, s32[]{:S(2)}) async-start(s8[8388608]{0:T(1024)(128)(4,1)} %bitcast.164), calls=%async_computation | async-start | bytes 8388608
  (26 other events, 118.9 us)
